TPU v7x, 512 devices: a whole 4x8x8 slice. The times are simulated.
512 devices in a mesh: section: 4 (over x_hi, core), feat: 128 (over y, z, x_lo).
Axes of the slice: x: 4 (x_hi: 2, x_lo: 2; x = x_hi * 2 + x_lo), y: 8, z: 8, core: 2. Of those that a mesh axis runs over, the one named last changes fastest.
Arguments:
- inputs: bfloat16 [4, 128, 8192], P('section', None, 'feat'), may hold values from -6 to 6
- targets: bfloat16 [4, 128, 8192], P('section', None, 'feat'), may hold values from -6 to 6
- enc_w: bfloat16 [4, 4096, 8192], P('section', 'feat'), may hold values from -0.0625 to 0.0625
- enc_b: float32 [4, 4096], P('section', 'feat'), may hold values from -3 to 3
- dec_w: bfloat16 [4, 2, 8192, 4096], P('section', None, 'feat'), may hold values from -0.375 to 0.375
- dec_b: float32 [4, 8192], P('section', 'feat'), may hold values from -3 to 3
Outputs:
- enc_grad: bfloat16 [4, 4096, 8192], P('section', 'feat')
- dec_grad: bfloat16 [4, 2, 8192, 4096], P('section', None, 'feat')
All inputs are finite; a program needn't handle non-finite values.
Results may differ from a plain program's by a relative error of at most 0.0058.
Values may be sent and summed in bfloat16 or wider, within the bound.
A program may use at most 64 MiB of HBM per device.

v0:
```python
import jax
import jax.numpy as jnp
from jax import lax
from jax.sharding import PartitionSpec as P


def from_behind(value, axis, steps):
    count = lax.axis_size(axis)
    initial, last = (max(0, -steps), min(count, count - steps))
    return lax.ppermute(value, axis, [(source, source + steps) for source in range(initial, last)])


def transposed(left, right):
    return lax.dot_general(
        left, right, (((0,), (0,)), ((), ())), preferred_element_type=jnp.float32
    )


def against(left, right):
    return lax.dot_general(
        left, right, (((1,), (1,)), ((), ())), preferred_element_type=jnp.float32
    )


def on_device(inputs, targets, enc_w, enc_b, dec_w, dec_b):
    scale = inputs.shape[1] ** (-0.5)
    reach = dec_w.shape[1]
    gathered = lax.all_gather(inputs[0], "feat", axis=1, tiled=True)
    pre = against(gathered, enc_w[0]) + enc_b[0]
    active = jnp.maximum(pre, 0.0)
    codes = (active * active).astype(jnp.bfloat16)
    own_codes = lax.all_gather(codes, "feat", axis=1, tiled=True)
    target = targets[0].astype(jnp.float32)
    weights = dec_w[0]
    code_grad = None
    sources = [own_codes]
    previous = own_codes
    previous = from_behind(previous, "section", 1)
    sources.append(previous)
    total = dec_b[0] + against(sources[0], weights[0])
    offset = 1
    total = total + against(sources[offset], weights[offset])
    error = ((total - target) * scale).astype(jnp.bfloat16)
    slots = [transposed(error, sources[offset]).astype(jnp.bfloat16) for offset in range(reach)]
    code_grad = jnp.dot(error, weights[0], preferred_element_type=jnp.float32)
    held_error = error
    held_weights = weights[1:]
    held_error, held_weights = from_behind((held_error, held_weights), "section", -1)
    code_grad = code_grad + jnp.dot(held_error, held_weights[0], preferred_element_type=jnp.float32)
    mine = lax.psum_scatter(code_grad, "feat", scatter_dimension=1, tiled=True)
    pre_grad = (mine * 2.0 * active).astype(jnp.bfloat16)
    enc_grad = transposed(pre_grad, gathered).astype(jnp.bfloat16)[None]
    dec_grad = jnp.stack(slots)[None]
    return (enc_grad, dec_grad)


def solution(mesh):
    return jax.shard_map(
        on_device,
        mesh=mesh,
        in_specs=(
            P("section", None, "feat"),
            P("section", None, "feat"),
            P("section", "feat", None),
            P("section", "feat"),
            P("section", None, "feat", None),
            P("section", "feat"),
        ),
        out_specs=(P("section", "feat", None), P("section", None, "feat", None)),
        check_vma=False,
    )
```

profile of v0, /device:TPU:4, one launch (start us, length us, event | category | flops | bytes accessed | tf_op | source)
XLA Modules:
  0.0 1848.6 jit_solution(361580426507441476)
XLA Ops:
  7.2 0.0 copy-start
  7.2 0.0 all-gather.6.cloned.1.call-start
  7.2 0.7 all-gather.6.cloned.1.call-update
  7.9 0.0 all-gather.4.cloned.1.call-start
  8.0 596.3 %all-gather.6.cloned.1.call-done = bf16[1,128,8192]{1,2,0:T(8,128)(2,1)} async-done(((bf16[1,128,64]{1,2,0:T(8,128)(2,1)}), bf16[1,128,8192]{1,2,0:T(8,128)(2,1)}) %all-gather.6.cloned.1.call-update) | async-done | bytes 2097168 | tf_op jit(solution)/shard_map/all_gather | solution.py:28
  604.3 2.7 multiply_convert_fusion.1
  607.0 0.0 all-gather.4.cloned.1.call-update
  607.0 0.0 reduce-scatter.2.cloned.1.call-start
  607.0 582.7 %all-gather.4.cloned.1.call-done = bf16[128,4096]{0,1:T(8,128)(2,1)} async-done(((bf16[128,32]{0,1:T(8,128)(2,1)}), bf16[128,4096]{0,1:T(8,128)(2,1)}) %all-gather.4.cloned.1.call-update) | async-done | bytes 1048592 | tf_op jit(solution)/shard_map/all_gather | solution.py:32
  1189.7 1.9 collective-permute-start
  1191.7 5.1 collective-permute-start.2
  1196.9 1.5 convolution_add_fusion.2
  1198.4 9.1 collective-permute-done
  1207.6 0.3 fusion.8
  1207.9 1.9 collective-permute-start.1
  1209.8 0.5 fusion.17
  1210.4 0.9 collective-permute-done.1
  1211.2 1.8 convolution_add_fusion
  1213.1 0.0 reduce-scatter.2.cloned.1.call-update
  1213.1 0.5 fusion.2
  1213.6 1.9 fusion.1
  1215.5 1.1 maximum_bitcast_fusion
  1216.5 623.2 %reduce-scatter.2.cloned.1.call-done = f32[128,32]{0,1:T(8,128)} async-done(((f32[128,4096]{0,1:T(8,128)}), f32[128,32]{0,1:T(8,128)}) %reduce-scatter.2.cloned.1.call-update) | async-done | bytes 16400 | tf_op jit(solution)/shard_map/reduce_scatter | solution.py:50
  1839.7 2.3 fusion
  (11 shorter events, 0.1 us)
Async XLA Ops:
  7.2 597.1 %copy-start = (bf16[1,32,8192]{2,1,0:T(8,128)(2,1)S(1)}, bf16[1,32,8192]{2,1,0:T(8,128)(2,1)}, u32[]{:S(2)}) copy-start(bf16[1,32,8192]{2,1,0:T(8,128)(2,1)} %param.8) | copy-start | bytes 1572868
  7.2 1184.5 %copy-start.2 = (bf16[1,2,64,4096]{3,2,1,0:T(8,128)(2,1)S(1)}, bf16[1,2,64,4096]{3,2,1,0:T(8,128)(2,1)}, u32[]{:S(2)}) copy-start(bf16[1,2,64,4096]{3,2,1,0:T(8,128)(2,1)} %param.10) | copy-start | bytes 3145732
  7.2 1189.7 %copy-start.4 = (f32[1,64]{1,0:T(1,128)S(1)}, f32[1,64]{1,0:T(1,128)}, u32[]{:S(2)}) copy-start(f32[1,64]{1,0:T(1,128)} %param.11) | copy-start | bytes 772
  7.2 597.1 %all-gather.6.cloned.1.call-start = ((), (), s32[]{:S(2)}) async-start(), calls=%async_computation.3 | async-start | bytes 2113536 | tf_op jit(solution)/shard_map/all_gather | solution.py:28
  7.9 1181.8 %all-gather.4.cloned.1.call-start = ((), (), s32[]{:S(2)}) async-start(), calls=%async_computation.1 | async-start | bytes 1056768 | tf_op jit(solution)/shard_map/all_gather | solution.py:32
  604.3 603.3 %copy-start.3 = (bf16[1,128,64]{1,2,0:T(8,128)(2,1)S(1)}, bf16[1,128,64]{1,2,0:T(8,128)(2,1)}, u32[]{:S(2)}) copy-start(bf16[1,128,64]{1,2,0:T(8,128)(2,1)} %param.7) | copy-start | bytes 49156
  607.0 1232.7 %reduce-scatter.2.cloned.1.call-start = ((), (), s32[]{:S(2)}) async-start(), calls=%async_computation.2 | async-start | bytes 2113536 | tf_op jit(solution)/shard_map/reduce_scatter | solution.py:50
  1189.7 17.8 collective-permute-start
  1191.7 18.6 %collective-permute-start.2 = (bf16[1,64,4096]{2,1,0:T(8,128)(2,1)S(1)}, bf16[1,64,4096]{2,1,0:T(8,128)(2,1)S(1)}, u32[]{:S(2)}, u32[]{:S(2)}) collective-permute-start(bf16[1,64,4096]{2,1,0:T(8,128)(2,1)S(1)} %slice_bitcast_fusion), channel_id=1, source_target_pairs={{128,0},{256,128},{384,256},{129,1},{257,129},{385,257},{130,2},{2... | collective-permute-start | bytes 1572872 | tf_op jit(solution)/shard_map/ppermute | solution.py:10
  1207.9 3.4 collective-permute-start.1
  1213.6 626.2 %copy-start.1 = (bf16[1,128,8192]{1,2,0:T(8,128)(2,1)S(1)}, bf16[1,128,8192]{1,2,0:T(8,128)(2,1)}, u32[]{:S(2)}) copy-start(bf16[1,128,8192]{1,2,0:T(8,128)(2,1)} %all-gather.6.cloned.1.call-done) | copy-start | bytes 6291460
Sparse Core Ops, SparseCore 0:
  10.1 594.1 all-gather.5
  607.1 582.5 all-gather.3
  1213.2 626.4 reduce-scatter.1
where the time goes:
time: 1850 us
  waiting for transfers between devices  1810 us (98%)
    reduce_scatter x1, waiting for transfers between devices, on_device(): mine = lax.psum_scatter(code_grad, 'feat', scatter_dimension=1, tiled=True)  623 us
    all_gather x1, waiting for transfers between devices, on_device(): gathered = lax.all_gather(inputs[0], 'feat', axis=1, tiled=True)  596 us
    all_gather x1, waiting for transfers between devices, on_device(): own_codes = lax.all_gather(codes, 'feat', axis=1, tiled=True)  583 us
  transfers between devices with their start and end apart: 6, of which 5 were waited for; matrix products, arithmetic and copies ran while one was open for 0% of the time, Pallas kernels for 0%

commit v1 on v0

--- a/solution.py
+++ b/solution.py
@@ -1,7 +1,18 @@
+import functools
 import jax
 import jax.numpy as jnp
 from jax import lax
 from jax.sharding import PartitionSpec as P
+
+
+def render_the_object(frame, group_axis):
+    taken_in = jax.lax.all_to_all(
+        jnp.stack([frame] * jax.lax.axis_size(group_axis), axis=0), group_axis, 0, 0
+    )
+    return jnp.concatenate(taken_in, axis=1)
+
+
+clusters_scan = functools.partial(render_the_object, group_axis="feat")
 
 
 def from_behind(value, axis, steps):
@@ -25,7 +36,7 @@
 def on_device(inputs, targets, enc_w, enc_b, dec_w, dec_b):
     scale = inputs.shape[1] ** (-0.5)
     reach = dec_w.shape[1]
-    gathered = lax.all_gather(inputs[0], "feat", axis=1, tiled=True)
+    gathered = clusters_scan(inputs[0])
     pre = against(gathered, enc_w[0]) + enc_b[0]
     active = jnp.maximum(pre, 0.0)
     codes = (active * active).astype(jnp.bfloat16)

time: 1850 us -> 1320 us (0.71)
  waiting for transfers between devices: 1810 us -> 1220 us
  blocking collectives: 0 us -> 70.2 us
    all_gather x1 -> x0, waiting for transfers between devices: 596 us -> none  [on_device(): gathered = lax.all_gather(inputs[0], 'feat', axis=1, tiled=True)]
    all_to_all x0 -> x1, blocking collectives: none -> 70.2 us  [render_the_object(): jax.lax.all_to_all(jnp.stack([frame] * jax.lax.axis_size(group_axis), axi...]
  transfers between devices with their start and end apart: 6 -> 5, of which waited for: 5 -> 4; matrix products, arithmetic and copies ran while one was open for 0% -> 1% of each run, Pallas kernels for 0% -> 0%
where the time goes in v1:
time: 1320 us
  waiting for transfers between devices  1220 us (92%)
  blocking collectives  70.2 us (5%)
  between operations  14.2 us (1%)
    reduce_scatter x1, waiting for transfers between devices, on_device(): mine = lax.psum_scatter(code_grad, 'feat', scatter_dimension=1, tiled=True)  623 us
    all_gather x1, waiting for transfers between devices, on_device(): own_codes = lax.all_gather(codes, 'feat', axis=1, tiled=True)  583 us
    all_to_all x1, blocking collectives, render_the_object(): jax.lax.all_to_all(jnp.stack([frame] * jax.lax.axis_size(group_axis), axi...  70.2 us
  transfers between devices with their start and end apart: 5, of which 4 were waited for; matrix products, arithmetic and copies ran while one was open for 1% of the time, Pallas kernels for 0%

profile of v1, /device:TPU:4, one launch (start us, length us, event | category | flops | bytes accessed | tf_op | source)
XLA Modules:
  0.0 1323.2 jit_solution(15397324210150074424)
XLA Ops:
  7.2 0.0 all-gather.2.cloned.1.call-start
  7.2 1.3 stack.12
  8.5 70.2 %all_to_all.5 = bf16[128,128,64]{1,2,0:T(8,128)(2,1)S(1)} all-to-all(bf16[128,128,64]{1,2,0:T(8,128)(2,1)S(1)} %stack.12), channel_id=1, replica_groups=mesh['section'=4,'feat'=128] {'feat'}, dimensions={0} | all-to-all | bytes 4194304 | tf_op jit(solution)/shard_map/all_to_all | solution.py:9
  78.8 1.1 multiply_convert_fusion.1
  79.8 0.0 all-gather.2.cloned.1.call-update
  79.8 0.0 reduce-scatter.2.cloned.1.call-start
  79.9 583.3 %all-gather.2.cloned.1.call-done = bf16[128,4096]{0,1:T(8,128)(2,1)} async-done(((bf16[128,32]{0,1:T(8,128)(2,1)}), bf16[128,4096]{0,1:T(8,128)(2,1)}) %all-gather.2.cloned.1.call-update) | async-done | bytes 1048592 | tf_op jit(solution)/shard_map/all_gather | solution.py:43
  663.2 2.0 collective-permute-start
  665.2 1.1 slice_bitcast_fusion
  666.3 5.1 collective-permute-start.2
  671.5 1.7 convolution_add_fusion.2
  673.2 7.9 collective-permute-done
  681.2 0.3 fusion.5
  681.5 0.6 copy-done.3
  682.1 1.9 collective-permute-start.1
  684.0 0.5 fusion.9
  684.6 0.9 collective-permute-done.1
  685.5 1.9 convolution_add_fusion
  687.3 0.0 reduce-scatter.2.cloned.1.call-update
  687.4 1.8 fusion.2
  689.2 0.5 fusion.1
  689.7 1.1 maximum_bitcast_fusion
  690.7 623.3 %reduce-scatter.2.cloned.1.call-done = f32[128,32]{0,1:T(8,128)} async-done(((f32[128,4096]{0,1:T(8,128)}), f32[128,32]{0,1:T(8,128)}) %reduce-scatter.2.cloned.1.call-update) | async-done | bytes 16400 | tf_op jit(solution)/shard_map/reduce_scatter | solution.py:61
  1314.0 2.3 fusion
  (14 shorter events, 0.0 us)
Async XLA Ops:
  7.2 71.6 %copy-start = (bf16[1,32,8192]{2,1,0:T(8,128)(2,1)S(1)}, bf16[1,32,8192]{2,1,0:T(8,128)(2,1)}, u32[]{:S(2)}) copy-start(bf16[1,32,8192]{2,1,0:T(8,128)(2,1)} %param.8) | copy-start | bytes 1572868
  7.2 656.0 %all-gather.2.cloned.1.call-start = ((), (), s32[]{:S(2)}) async-start(), calls=%async_computation.2 | async-start | bytes 1056768 | tf_op jit(solution)/shard_map/all_gather | solution.py:43
  8.5 70.2 %copy-start.6 = (f32[1,32]{1,0:T(1,128)S(1)}, f32[1,32]{1,0:T(1,128)}, u32[]{:S(2)}) copy-start(f32[1,32]{1,0:T(1,128)} %param.9) | copy-start | bytes 388
  78.7 592.7 %copy-start.5 = (f32[1,64]{1,0:T(1,128)S(1)}, f32[1,64]{1,0:T(1,128)}, u32[]{:S(2)}) copy-start(f32[1,64]{1,0:T(1,128)} %param.11) | copy-start | bytes 772
  78.7 602.4 %copy-start.4 = (bf16[1,128,64]{1,2,0:T(8,128)(2,1)S(1)}, bf16[1,128,64]{1,2,0:T(8,128)(2,1)}, u32[]{:S(2)}) copy-start(bf16[1,128,64]{1,2,0:T(8,128)(2,1)} %param.7) | copy-start | bytes 49156
  79.8 1234.2 %reduce-scatter.2.cloned.1.call-start = ((), (), s32[]{:S(2)}) async-start(), calls=%async_computation.3 | async-start | bytes 2113536 | tf_op jit(solution)/shard_map/reduce_scatter | solution.py:61
  663.2 18.0 %copy-start.1 = (bf16[1,2,64,4096]{3,2,1,0:T(8,128)(2,1)S(1)}, bf16[1,2,64,4096]{3,2,1,0:T(8,128)(2,1)}, u32[]{:S(2)}) copy-start(bf16[1,2,64,4096]{3,2,1,0:T(8,128)(2,1)} %param.10) | copy-start | bytes 3145732
  663.2 18.0 %collective-permute-start = (bf16[128,4096]{0,1:T(8,128)(2,1)}, bf16[128,4096]{0,1:T(8,128)(2,1)S(1)}, u32[]{:S(2)}, u32[]{:S(2)}) collective-permute-start(bf16[128,4096]{0,1:T(8,128)(2,1)} %all-gather.2.cloned.1.call-done), channel_id=1, source_target_pairs={{0,128},{128,256},{256,384},{1,129},{129,257},{257,385},{2,130},{1... | collective-permute-start | bytes 3145736 | tf_op jit(solution)/shard_map/ppermute | solution.py:21
  666.3 18.3 %collective-permute-start.2 = (bf16[1,64,4096]{2,1,0:T(8,128)(2,1)S(1)}, bf16[1,64,4096]{2,1,0:T(8,128)(2,1)S(1)}, u32[]{:S(2)}, u32[]{:S(2)}) collective-permute-start(bf16[1,64,4096]{2,1,0:T(8,128)(2,1)S(1)} %slice_bitcast_fusion), channel_id=1, source_target_pairs={{128,0},{256,128},{384,256},{129,1},{257,129},{385,257},{130,2},{2... | collective-permute-start | bytes 1572872 | tf_op jit(solution)/shard_map/ppermute | solution.py:21
  681.1 1.0 copy-start.3
  682.1 3.3 collective-permute-start.1
  687.4 1.8 copy-start.2
Sparse Core Ops, SparseCore 0:
  80.0 583.1 all-gather.1
  687.5 626.4 reduce-scatter.1
